TPU v7x, 128 devices: a whole 4x4x4 slice. The times are simulated.
128 devices in a mesh: tm: 8 (over y_hi, z), rows: 16 (over y_lo, x, core).
Axes of the slice: x: 4, y: 4 (y_hi: 2, y_lo: 2; y = y_hi * 2 + y_lo), z: 4, core: 2. Of those that a mesh axis runs over, the one named last changes fastest.
Arguments:
- video: bfloat16 [1, 32, 128, 128, 256], P(None, 'tm', 'rows'), may hold values from -6 to 6
- spatial_weight: bfloat16 [2304, 256], P(('tm', 'rows')), may hold values from -0.125 to 0.125
- temporal_weight: bfloat16 [768, 256], P(('tm', 'rows')), may hold values from -0.21875 to 0.21875
- cotangent: bfloat16 [1, 32, 128, 128, 256], P(None, 'tm', 'rows'), may hold values from -6 to 6
Outputs:
- output: bfloat16 [1, 32, 128, 128, 256], P(None, 'tm', 'rows')
- grad_video: bfloat16 [1, 32, 128, 128, 256], P(None, 'tm', 'rows')
- grad_spatial: float32 [2304, 256], P(('tm', 'rows'))
- grad_temporal: float32 [768, 256], P(('tm', 'rows'))
All inputs are finite; a program needn't handle non-finite values.
Results may differ from a plain program's by a relative error of at most 0.0053.
Values may be sent and summed in bfloat16 or wider, within the bound.
No kernel may reach another device: no remote copies, remote signals or barrier semaphores. Data moves between devices by JAX's collectives and lax.ppermute only.
A program may use at most 128 MiB of HBM per device.

v0:
```python
import jax
import jax.numpy as jnp
from jax import lax
from jax.sharding import PartitionSpec as P

epsilon = 1e-06


def with_halo(x, sides, width):
    for axis, dim in sides:
        count, length = (lax.axis_size(axis), x.shape[dim])
        up = [(i, (i + 1) % count) for i in range(count - 1)]
        down = [(j, i) for i, j in up]
        last = lax.slice_in_dim(x, length - width, length, axis=dim)
        leading = lax.slice_in_dim(x, 0, width, axis=dim)
        before = lax.ppermute(last, axis, up)
        after = lax.ppermute(leading, axis, down)
        x = jnp.concatenate([before, x, after], axis=dim)
    return x


def passed_along(x, axis, by):
    count = lax.axis_size(axis)
    pairs = [(i, i + by) for i in range(count) if 0 <= i + by < count]
    return lax.ppermute(x, axis, pairs)


def rim_pad(field):
    rimmed = with_halo(field, (("rows", 2),), 1)
    return jnp.pad(rimmed, ((0, 0), (0, 0), (0, 0), (1, 1), (0, 0)))


def shifted_view(padded, tap_row, tap_col, n_rows, n_cols):
    chans = padded.shape[-1]
    return padded[:, :, tap_row : tap_row + n_rows, tap_col : tap_col + n_cols].reshape(-1, chans)


def conv_three(padded, weight, n_rows, n_cols):
    chans = padded.shape[-1]
    total = None
    for tap_row in range(3):
        for tap_col in range(3):
            block = weight[(3 * tap_row + tap_col) * chans : (3 * tap_row + tap_col + 1) * chans]
            term = jnp.dot(
                shifted_view(padded, tap_row, tap_col, n_rows, n_cols),
                block,
                preferred_element_type=jnp.float32,
            )
            total = term if total is None else total + term
    return total


def kernel_grad(padded, grad_flat, n_rows, n_cols):
    blocks = [
        contract(shifted_view(padded, tap_row, tap_col, n_rows, n_cols), grad_flat)
        for tap_row in range(3)
        for tap_col in range(3)
    ]
    return jnp.concatenate(blocks, axis=0)


def frame_cols(padded, n_frames):
    chans = padded.shape[-1]
    return jnp.concatenate([padded[:, k : k + n_frames] for k in range(3)], axis=-1).reshape(
        -1, 3 * chans
    )


def silu_slope(value):
    sigmoid = jax.nn.sigmoid(value)
    return sigmoid * (1.0 + value * (1.0 - sigmoid))


def contract(left, right):
    return lax.dot_general(
        left, right, (((0,), (0,)), ((), ())), preferred_element_type=jnp.float32
    )


def reverse_spatial(weight, chans):
    return (
        weight.reshape(3, 3, chans, chans)[::-1, ::-1]
        .transpose(0, 1, 3, 2)
        .reshape(9 * chans, chans)
    )


def reverse_temporal(weight, chans):
    return weight.reshape(3, chans, chans)[::-1].transpose(0, 2, 1).reshape(3 * chans, chans)


def shards(video, spatial_weight, temporal_weight, cotangent):
    n_batch, n_frames, n_rows, n_cols, chans = video.shape
    full_spatial, full_temporal = (
        lax.all_gather(spatial_weight, ("tm", "rows"), axis=0, tiled=True),
        lax.all_gather(temporal_weight, ("tm", "rows"), axis=0, tiled=True),
    )
    values = video.astype(jnp.float32)
    inv_rms = lax.rsqrt(jnp.mean(values * values, axis=-1, keepdims=True) + epsilon)
    normed = values * inv_rms
    activated = jax.nn.silu(normed).astype(jnp.bfloat16)
    padded_act = rim_pad(activated)
    pre_act = conv_three(padded_act, full_spatial, n_rows, n_cols).reshape(video.shape)
    hidden = jax.nn.silu(pre_act).astype(jnp.bfloat16)
    back_temporal = reverse_temporal(full_temporal, chans)
    past = passed_along(hidden[:, n_frames - 2 :], "tm", 1)
    ahead = passed_along(cotangent[:, :2], "tm", -1)
    from_past = frame_cols(jnp.concatenate([past, hidden], axis=1), n_frames)
    from_ahead = frame_cols(jnp.concatenate([cotangent, ahead], axis=1), n_frames)
    mixed = jnp.dot(from_past, full_temporal, preferred_element_type=jnp.float32).reshape(
        video.shape
    )
    back = jnp.dot(from_ahead, back_temporal, preferred_element_type=jnp.float32).reshape(
        video.shape
    )
    grad_temporal = contract(from_past, cotangent.reshape(-1, chans))
    output = (values + mixed).astype(jnp.bfloat16)
    grad_pre = (back * silu_slope(pre_act)).astype(jnp.bfloat16)
    grad_spatial = kernel_grad(padded_act, grad_pre.reshape(-1, chans), n_rows, n_cols)
    back_spatial = reverse_spatial(full_spatial, chans)
    grad_act = conv_three(rim_pad(grad_pre), back_spatial, n_rows, n_cols).reshape(video.shape)
    grad_norm = grad_act * silu_slope(normed)
    grad_in = inv_rms * (grad_norm - normed * jnp.mean(grad_norm * normed, axis=-1, keepdims=True))
    grad_video = (cotangent.astype(jnp.float32) + grad_in).astype(jnp.bfloat16)
    spatial_part, temporal_part = (
        lax.psum_scatter(grad_spatial, ("tm", "rows"), scatter_dimension=0, tiled=True),
        lax.psum_scatter(grad_temporal, ("tm", "rows"), scatter_dimension=0, tiled=True),
    )
    total_cells = n_batch * n_frames * n_rows * n_cols * lax.axis_size("tm") * lax.axis_size("rows")
    factor = float(total_cells) ** (-0.5)
    return (output, grad_video, spatial_part * factor, temporal_part * factor)


def solution(mesh):
    in_specs = (
        P(None, "tm", "rows", None, None),
        P(("tm", "rows"), None),
        P(("tm", "rows"), None),
        P(None, "tm", "rows", None, None),
    )
    out_specs = (
        P(None, "tm", "rows", None, None),
        P(None, "tm", "rows", None, None),
        P(("tm", "rows"), None),
        P(("tm", "rows"), None),
    )
    return jax.shard_map(shards, mesh=mesh, in_specs=in_specs, out_specs=out_specs, check_vma=False)
```

profile of v0, /device:TPU:4, one launch (start us, length us, event | category | flops | bytes accessed | tf_op | source)
XLA Modules:
  0.0 832.9 jit_solution(6420278015430662452)
XLA Ops:
  7.9 2.4 fusion.32
  14.4 3.6 collective-permute-start.1
  20.5 175.8 %all-gather.1 = bf16[128,6,256]{2,1,0:T(8,128)(2,1)S(1)} all-gather(bf16[1,6,256]{2,1,0:T(8,128)(2,1)S(1)} %bitcast.245), channel_id=1, replica_groups=mesh['tm'=8,'rows'=16] {'tm','rows'}, dimensions={0}, use_global_device_ids=true | all-gather | bytes 396288 | tf_op jit(solution)/shard_map/all_gather | solution.py:96
  200.0 2.3 pad_maximum_fusion.3
  203.9 5.4 fusion.149
  210.6 2.5 fusion.147
  213.2 8.5 %all-gather.4.cloned.1.call-done = bf16[128,18,256]{2,1,0:T(8,128)(2,1)} async-done(((bf16[1,18,256]{2,1,0:T(8,128)(2,1)}), bf16[128,18,256]{2,1,0:T(8,128)(2,1)}) %all-gather.4.cloned.1.call-update) | async-done | bytes 1179664 | tf_op jit(solution)/shard_map/all_gather | solution.py:95
  221.6 2.3 reshape.272
  224.0 2.4 fusion.135
  236.7 2.7 multiply_convert_fusion.1
  241.6 6.7 collective-permute-start.2
  248.4 3.2 multiply_convert_fusion
  262.8 3.6 collective-permute-start.5
  266.5 3.4 reshape.249
  272.7 3.1 fusion.111
  275.8 2.3 select_maximum_fusion
  278.1 3.2 pad_maximum_fusion.1
  281.4 4.6 fusion.148
  285.9 2.8 fusion.124
  291.6 3.8 fusion.57
  295.4 328.1 %fusion.146 = (f32[24,256]{1,0:T(8,128)S(1)}, f32[8,256]{1,0:T(8,128)S(1)}) fusion(f32[2304,256]{1,0:T(8,128)} %fusion.111, f32[768,256]{1,0:T(8,128)} %fusion.57), kind=kCustom, calls=%all-reduce-scatter.2 | all-reduce-scatter fusion | flops 1048578 | bytes 3178496
  623.4 1.9 collective-permute-start.38
  625.4 1.9 collective-permute-start.39
  627.3 1.9 collective-permute-start.40
  630.5 3.7 convolution_add_fusion.6
  634.2 1.9 collective-permute-start.41
  640.1 3.7 collective-permute-done.40
  645.9 4.9 collective-permute-done.41
  650.8 10.5 %collective-permute-start.46 = (f32[8,256]{1,0:T(8,128)S(1)}, f32[8,256]{1,0:T(8,128)S(1)}, u32[]{:S(2)}, u32[]{:S(2)}) collective-permute-start(f32[8,256]{1,0:T(8,128)S(1)} %get-tuple-element.7), channel_id=1, source_target_pairs={{0,9},{1,10},{2,11},{3,12},{4,13},{5,14},{6,15},{7,16},{8,17},{9,1... | collective-permute-start | bytes 24584
  661.3 3.1 collective-permute-start.47
  667.4 18.3 %collective-permute-start.50 = (f32[8,256]{1,0:T(8,128)S(1)}, f32[8,256]{1,0:T(8,128)S(1)}, u32[]{:S(2)}, u32[]{:S(2)}) collective-permute-start(f32[8,256]{1,0:T(8,128)S(1)} %get-tuple-element.7), channel_id=1, source_target_pairs={{0,13},{1,14},{2,15},{3,16},{4,17},{5,18},{6,19},{7,20},{8,21},{9,... | collective-permute-start | bytes 24584
  686.5 2.9 collective-permute-start.51
  689.4 1.9 collective-permute-start.52
  695.2 3.1 collective-permute-start.55
  699.1 3.8 collective-permute-start.56
  710.0 2.2 collective-permute-start.61
  713.9 2.8 collective-permute-start.63
  718.4 2.4 collective-permute-start.65
  725.9 4.0 collective-permute-start.10
  733.7 2.1 collective-permute-start.12
  735.9 4.1 collective-permute-start.13
  740.0 1.9 collective-permute-start.14
  742.0 3.7 collective-permute-start.15
  746.5 1.9 collective-permute-start.16
  748.5 2.9 collective-permute-start.17
  751.4 2.7 collective-permute-start.18
  754.2 3.9 collective-permute-start.19
  759.8 2.4 fusion.27
  764.8 2.6 collective-permute-start.23
  767.4 3.5 collective-permute-start.24
  772.7 1.9 collective-permute-start.26
  774.6 2.0 collective-permute-start.27
  778.1 2.3 collective-permute-start.29
  782.1 3.7 fusion.31
  785.8 2.8 collective-permute-start.31
  790.2 2.0 collective-permute-start.33
  793.6 2.2 collective-permute-start.35
  796.0 4.1 fusion.33
  800.3 2.9 concatenate.53
  806.5 2.7 collective-permute-start.7
  809.2 4.5 collective-permute-start.8
  813.7 1.9 collective-permute-start.9
  816.3 4.7 collective-permute-done.9
  820.9 4.3 concatenate.52
  (294 shorter events, 94.9 us)
Async XLA Ops:
  7.2 214.5 %all-gather.4.cloned.1.call-start = ((), (), s32[]{:S(2)}) async-start(), calls=%async_computation | async-start | bytes 1585152 | tf_op jit(solution)/shard_map/all_gather | solution.py:95
  12.5 187.5 %collective-permute-start = (bf16[1,4,1,128,256]{4,3,2,1,0:T(8,128)(2,1)}, bf16[1,4,1,128,256]{4,3,2,1,0:T(8,128)(2,1)S(1)}, u32[]{:S(2)}, u32[]{:S(2)}) collective-permute-start(bf16[1,4,1,128,256]{4,3,2,1,0:T(8,128)(2,1)} %get-tuple-element.28), channel_id=1, source_target_pairs={{0,1},{1,2},{2,3},{3,4},{4,5},{5,6},{6,7},{7,8},{8,9},{9,10},{10,1... | collective-permute-start | bytes 786440 | tf_op jit(solution)/shard_map/ppermute | solution.py:16
  14.4 185.5 %collective-permute-start.1 = (bf16[1,4,1,128,256]{4,3,2,1,0:T(8,128)(2,1)}, bf16[1,4,1,128,256]{4,3,2,1,0:T(8,128)(2,1)S(1)}, u32[]{:S(2)}, u32[]{:S(2)}) collective-permute-start(bf16[1,4,1,128,256]{4,3,2,1,0:T(8,128)(2,1)} %get-tuple-element.29), channel_id=1, source_target_pairs={{1,0},{2,1},{3,2},{4,3},{5,4},{6,5},{7,6},{8,7},{9,8},{10,9},{11,1... | collective-permute-start | bytes 786440 | tf_op jit(solution)/shard_map/ppermute | solution.py:17
  19.2 190.2 %collective-permute-start.3 = (bf16[1,2,8,128,256]{4,3,2,1,0:T(8,128)(2,1)}, bf16[1,2,8,128,256]{4,3,2,1,0:T(8,128)(2,1)}, u32[]{:S(2)}, u32[]{:S(2)}) collective-permute-start(bf16[1,2,8,128,256]{4,3,2,1,0:T(8,128)(2,1)} %slice.175), channel_id=1, source_target_pairs={{16,0},{32,16},{48,32},{64,48},{80,64},{96,80},{112,96},{17,1},{33... | collective-permute-start | bytes 3145736 | tf_op jit(solution)/shard_map/ppermute | solution.py:25
  241.6 47.1 %collective-permute-start.2 = (bf16[1,2,8,128,256]{4,3,2,1,0:T(8,128)(2,1)}, bf16[1,2,8,128,256]{4,3,2,1,0:T(8,128)(2,1)}, u32[]{:S(2)}, u32[]{:S(2)}) collective-permute-start(bf16[1,2,8,128,256]{4,3,2,1,0:T(8,128)(2,1)} %slice.214), channel_id=1, source_target_pairs={{0,16},{16,32},{32,48},{48,64},{64,80},{80,96},{96,112},{1,17},{17... | collective-permute-start | bytes 3145736 | tf_op jit(solution)/shard_map/ppermute | solution.py:25
  260.9 14.9 %collective-permute-start.4 = (bf16[1,4,1,128,256]{4,3,2,1,0:T(8,128)(2,1)}, bf16[1,4,1,128,256]{4,3,2,1,0:T(8,128)(2,1)S(1)}, u32[]{:S(2)}, u32[]{:S(2)}) collective-permute-start(bf16[1,4,1,128,256]{4,3,2,1,0:T(8,128)(2,1)} %get-tuple-element.24), channel_id=1, source_target_pairs={{0,1},{1,2},{2,3},{3,4},{4,5},{5,6},{6,7},{7,8},{8,9},{9,10},{10,1... | collective-permute-start | bytes 786440 | tf_op jit(solution)/shard_map/ppermute | solution.py:16
  262.8 13.0 %collective-permute-start.5 = (bf16[1,4,1,128,256]{4,3,2,1,0:T(8,128)(2,1)}, bf16[1,4,1,128,256]{4,3,2,1,0:T(8,128)(2,1)}, u32[]{:S(2)}, u32[]{:S(2)}) collective-permute-start(bf16[1,4,1,128,256]{4,3,2,1,0:T(8,128)(2,1)} %get-tuple-element.25), channel_id=1, source_target_pairs={{1,0},{2,1},{3,2},{4,3},{5,4},{6,5},{7,6},{8,7},{9,8},{10,9},{11,1... | collective-permute-start | bytes 786440 | tf_op jit(solution)/shard_map/ppermute | solution.py:17
  623.4 14.0 %collective-permute-start.38 = (f32[8,256]{1,0:T(8,128)S(1)}, f32[8,256]{1,0:T(8,128)S(1)}, u32[]{:S(2)}, u32[]{:S(2)}) collective-permute-start(f32[8,256]{1,0:T(8,128)S(1)} %get-tuple-element.7), channel_id=1, source_target_pairs={{0,1},{1,2},{2,3},{3,4},{4,5},{5,6},{6,7},{7,8},{8,9},{9,10},{10,1... | collective-permute-start | bytes 24584
  625.4 13.4 %collective-permute-start.39 = (f32[8,256]{1,0:T(8,128)S(1)}, f32[8,256]{1,0:T(8,128)S(1)}, u32[]{:S(2)}, u32[]{:S(2)}) collective-permute-start(f32[8,256]{1,0:T(8,128)S(1)} %get-tuple-element.7), channel_id=1, source_target_pairs={{0,2},{1,3},{2,4},{3,5},{4,6},{5,7},{6,8},{7,9},{8,10},{9,11},{10,... | collective-permute-start | bytes 24584
  627.3 16.5 %collective-permute-start.40 = (f32[8,256]{1,0:T(8,128)S(1)}, f32[8,256]{1,0:T(8,128)S(1)}, u32[]{:S(2)}, u32[]{:S(2)}) collective-permute-start(f32[8,256]{1,0:T(8,128)S(1)} %get-tuple-element.7), channel_id=1, source_target_pairs={{0,3},{1,4},{2,5},{3,6},{4,7},{5,8},{6,9},{7,10},{8,11},{9,12},{10... | collective-permute-start | bytes 24584
  634.2 16.6 %collective-permute-start.41 = (f32[8,256]{1,0:T(8,128)S(1)}, f32[8,256]{1,0:T(8,128)S(1)}, u32[]{:S(2)}, u32[]{:S(2)}) collective-permute-start(f32[8,256]{1,0:T(8,128)S(1)} %get-tuple-element.7), channel_id=1, source_target_pairs={{0,4},{1,5},{2,6},{3,7},{4,8},{5,9},{6,10},{7,11},{8,12},{9,13},{1... | collective-permute-start | bytes 24584
  636.2 25.1 %collective-permute-start.42 = (f32[8,256]{1,0:T(8,128)S(1)}, f32[8,256]{1,0:T(8,128)S(1)}, u32[]{:S(2)}, u32[]{:S(2)}) collective-permute-start(f32[8,256]{1,0:T(8,128)S(1)} %get-tuple-element.7), channel_id=1, source_target_pairs={{0,5},{1,6},{2,7},{3,8},{4,9},{5,10},{6,11},{7,12},{8,13},{9,14},{... | collective-permute-start | bytes 24584
  637.5 26.9 %collective-permute-start.43 = (f32[8,256]{1,0:T(8,128)S(1)}, f32[8,256]{1,0:T(8,128)S(1)}, u32[]{:S(2)}, u32[]{:S(2)}) collective-permute-start(f32[8,256]{1,0:T(8,128)S(1)} %get-tuple-element.7), channel_id=1, source_target_pairs={{0,6},{1,7},{2,8},{3,9},{4,10},{5,11},{6,12},{7,13},{8,14},{9,15},... | collective-permute-start | bytes 24584
  638.8 26.9 %collective-permute-start.44 = (f32[8,256]{1,0:T(8,128)S(1)}, f32[8,256]{1,0:T(8,128)S(1)}, u32[]{:S(2)}, u32[]{:S(2)}) collective-permute-start(f32[8,256]{1,0:T(8,128)S(1)} %get-tuple-element.7), channel_id=1, source_target_pairs={{0,7},{1,8},{2,9},{3,10},{4,11},{5,12},{6,13},{7,14},{8,15},{9,16}... | collective-permute-start | bytes 24584
  643.8 23.5 %collective-permute-start.45 = (f32[8,256]{1,0:T(8,128)S(1)}, f32[8,256]{1,0:T(8,128)S(1)}, u32[]{:S(2)}, u32[]{:S(2)}) collective-permute-start(f32[8,256]{1,0:T(8,128)S(1)} %get-tuple-element.7), channel_id=1, source_target_pairs={{0,8},{1,9},{2,10},{3,11},{4,12},{5,13},{6,14},{7,15},{8,16},{9,17... | collective-permute-start | bytes 24584
  650.8 35.7 %collective-permute-start.46 = (f32[8,256]{1,0:T(8,128)S(1)}, f32[8,256]{1,0:T(8,128)S(1)}, u32[]{:S(2)}, u32[]{:S(2)}) collective-permute-start(f32[8,256]{1,0:T(8,128)S(1)} %get-tuple-element.7), channel_id=1, source_target_pairs={{0,9},{1,10},{2,11},{3,12},{4,13},{5,14},{6,15},{7,16},{8,17},{9,1... | collective-permute-start | bytes 24584
  661.3 28.1 %collective-permute-start.47 = (f32[8,256]{1,0:T(8,128)S(1)}, f32[8,256]{1,0:T(8,128)S(1)}, u32[]{:S(2)}, u32[]{:S(2)}) collective-permute-start(f32[8,256]{1,0:T(8,128)S(1)} %get-tuple-element.7), channel_id=1, source_target_pairs={{0,10},{1,11},{2,12},{3,13},{4,14},{5,15},{6,16},{7,17},{8,18},{9,... | collective-permute-start | bytes 24584
  664.4 27.0 %collective-permute-start.48 = (f32[8,256]{1,0:T(8,128)S(1)}, f32[8,256]{1,0:T(8,128)S(1)}, u32[]{:S(2)}, u32[]{:S(2)}) collective-permute-start(f32[8,256]{1,0:T(8,128)S(1)} %get-tuple-element.7), channel_id=1, source_target_pairs={{0,11},{1,12},{2,13},{3,14},{4,15},{5,16},{6,17},{7,18},{8,19},{9,... | collective-permute-start | bytes 24584
  665.7 27.5 %collective-permute-start.49 = (f32[8,256]{1,0:T(8,128)S(1)}, f32[8,256]{1,0:T(8,128)S(1)}, u32[]{:S(2)}, u32[]{:S(2)}) collective-permute-start(f32[8,256]{1,0:T(8,128)S(1)} %get-tuple-element.7), channel_id=1, source_target_pairs={{0,12},{1,13},{2,14},{3,15},{4,16},{5,17},{6,18},{7,19},{8,20},{9,... | collective-permute-start | bytes 24584
  667.4 27.7 %collective-permute-start.50 = (f32[8,256]{1,0:T(8,128)S(1)}, f32[8,256]{1,0:T(8,128)S(1)}, u32[]{:S(2)}, u32[]{:S(2)}) collective-permute-start(f32[8,256]{1,0:T(8,128)S(1)} %get-tuple-element.7), channel_id=1, source_target_pairs={{0,13},{1,14},{2,15},{3,16},{4,17},{5,18},{6,19},{7,20},{8,21},{9,... | collective-permute-start | bytes 24584
  686.5 12.6 %collective-permute-start.51 = (f32[8,256]{1,0:T(8,128)S(1)}, f32[8,256]{1,0:T(8,128)S(1)}, u32[]{:S(2)}, u32[]{:S(2)}) collective-permute-start(f32[8,256]{1,0:T(8,128)S(1)} %get-tuple-element.7), channel_id=1, source_target_pairs={{0,14},{1,15},{2,16},{3,17},{4,18},{5,19},{6,20},{7,21},{8,22},{9,... | collective-permute-start | bytes 24584
  689.4 13.5 %collective-permute-start.52 = (f32[8,256]{1,0:T(8,128)S(1)}, f32[8,256]{1,0:T(8,128)S(1)}, u32[]{:S(2)}, u32[]{:S(2)}) collective-permute-start(f32[8,256]{1,0:T(8,128)S(1)} %get-tuple-element.7), channel_id=1, source_target_pairs={{0,15},{1,16},{2,17},{3,18},{4,19},{5,20},{6,21},{7,22},{8,23},{9,... | collective-permute-start | bytes 24584
  691.4 13.2 %collective-permute-start.53 = (f32[8,256]{1,0:T(8,128)S(1)}, f32[8,256]{1,0:T(8,128)S(1)}, u32[]{:S(2)}, u32[]{:S(2)}) collective-permute-start(f32[8,256]{1,0:T(8,128)S(1)} %get-tuple-element.7), channel_id=1, source_target_pairs={{0,16},{1,17},{2,18},{3,19},{4,20},{5,21},{6,22},{7,23},{8,24},{9,... | collective-permute-start | bytes 24584
  693.2 13.0 %collective-permute-start.54 = (f32[8,256]{1,0:T(8,128)S(1)}, f32[8,256]{1,0:T(8,128)S(1)}, u32[]{:S(2)}, u32[]{:S(2)}) collective-permute-start(f32[8,256]{1,0:T(8,128)S(1)} %get-tuple-element.7), channel_id=1, source_target_pairs={{0,17},{1,18},{2,19},{3,20},{4,21},{5,22},{6,23},{7,24},{8,25},{9,... | collective-permute-start | bytes 24584
  695.2 12.4 %collective-permute-start.55 = (f32[8,256]{1,0:T(8,128)S(1)}, f32[8,256]{1,0:T(8,128)S(1)}, u32[]{:S(2)}, u32[]{:S(2)}) collective-permute-start(f32[8,256]{1,0:T(8,128)S(1)} %get-tuple-element.7), channel_id=1, source_target_pairs={{0,18},{1,19},{2,20},{3,21},{4,22},{5,23},{6,24},{7,25},{8,26},{9,... | collective-permute-start | bytes 24584
  699.1 10.9 %collective-permute-start.56 = (f32[8,256]{1,0:T(8,128)S(1)}, f32[8,256]{1,0:T(8,128)S(1)}, u32[]{:S(2)}, u32[]{:S(2)}) collective-permute-start(f32[8,256]{1,0:T(8,128)S(1)} %get-tuple-element.7), channel_id=1, source_target_pairs={{0,19},{1,20},{2,21},{3,22},{4,23},{5,24},{6,25},{7,26},{8,27},{9,... | collective-permute-start | bytes 24584
  706.2 10.5 %collective-permute-start.59 = (f32[8,256]{1,0:T(8,128)S(1)}, f32[8,256]{1,0:T(8,128)S(1)}, u32[]{:S(2)}, u32[]{:S(2)}) collective-permute-start(f32[8,256]{1,0:T(8,128)S(1)} %get-tuple-element.7), channel_id=1, source_target_pairs={{0,22},{1,23},{2,24},{3,25},{4,26},{5,27},{6,28},{7,29},{8,30},{9,... | collective-permute-start | bytes 24584
  707.6 10.8 %collective-permute-start.60 = (f32[8,256]{1,0:T(8,128)S(1)}, f32[8,256]{1,0:T(8,128)S(1)}, u32[]{:S(2)}, u32[]{:S(2)}) collective-permute-start(f32[8,256]{1,0:T(8,128)S(1)} %get-tuple-element.7), channel_id=1, source_target_pairs={{0,23},{1,24},{2,25},{3,26},{4,27},{5,28},{6,29},{7,30},{8,31},{9,... | collective-permute-start | bytes 24584
  710.0 11.5 %collective-permute-start.61 = (f32[8,256]{1,0:T(8,128)S(1)}, f32[8,256]{1,0:T(8,128)S(1)}, u32[]{:S(2)}, u32[]{:S(2)}) collective-permute-start(f32[8,256]{1,0:T(8,128)S(1)} %get-tuple-element.7), channel_id=1, source_target_pairs={{0,24},{1,25},{2,26},{3,27},{4,28},{5,29},{6,30},{7,31},{8,32},{9,... | collective-permute-start | bytes 24584
  712.3 11.0 %collective-permute-start.62 = (f32[8,256]{1,0:T(8,128)S(1)}, f32[8,256]{1,0:T(8,128)S(1)}, u32[]{:S(2)}, u32[]{:S(2)}) collective-permute-start(f32[8,256]{1,0:T(8,128)S(1)} %get-tuple-element.7), channel_id=1, source_target_pairs={{0,25},{1,26},{2,27},{3,28},{4,29},{5,30},{6,31},{7,32},{8,33},{9,... | collective-permute-start | bytes 24584
  713.9 10.6 %collective-permute-start.63 = (f32[8,256]{1,0:T(8,128)S(1)}, f32[8,256]{1,0:T(8,128)S(1)}, u32[]{:S(2)}, u32[]{:S(2)}) collective-permute-start(f32[8,256]{1,0:T(8,128)S(1)} %get-tuple-element.7), channel_id=1, source_target_pairs={{0,26},{1,27},{2,28},{3,29},{4,30},{5,31},{6,32},{7,33},{8,34},{9,... | collective-permute-start | bytes 24584
  718.4 11.5 %collective-permute-start.65 = (f32[8,256]{1,0:T(8,128)S(1)}, f32[8,256]{1,0:T(8,128)S(1)}, u32[]{:S(2)}, u32[]{:S(2)}) collective-permute-start(f32[8,256]{1,0:T(8,128)S(1)} %get-tuple-element.7), channel_id=1, source_target_pairs={{0,28},{1,29},{2,30},{3,31},{4,32},{5,33},{6,34},{7,35},{8,36},{9,... | collective-permute-start | bytes 24584
  721.6 10.4 %collective-permute-start.66 = (f32[8,256]{1,0:T(8,128)S(1)}, f32[8,256]{1,0:T(8,128)S(1)}, u32[]{:S(2)}, u32[]{:S(2)}) collective-permute-start(f32[8,256]{1,0:T(8,128)S(1)} %get-tuple-element.7), channel_id=1, source_target_pairs={{0,29},{1,30},{2,31},{3,32},{4,33},{5,34},{6,35},{7,36},{8,37},{9,... | collective-permute-start | bytes 24584
  723.2 10.5 %collective-permute-start.67 = (f32[8,256]{1,0:T(8,128)S(1)}, f32[8,256]{1,0:T(8,128)S(1)}, u32[]{:S(2)}, u32[]{:S(2)}) collective-permute-start(f32[8,256]{1,0:T(8,128)S(1)} %get-tuple-element.7), channel_id=1, source_target_pairs={{0,30},{1,31},{2,32},{3,33},{4,34},{5,35},{6,36},{7,37},{8,38},{9,... | collective-permute-start | bytes 24584
  724.5 11.3 %collective-permute-start.68 = (f32[8,256]{1,0:T(8,128)S(1)}, f32[8,256]{1,0:T(8,128)S(1)}, u32[]{:S(2)}, u32[]{:S(2)}) collective-permute-start(f32[8,256]{1,0:T(8,128)S(1)} %get-tuple-element.7), channel_id=1, source_target_pairs={{0,31},{1,32},{2,33},{3,34},{4,35},{5,36},{6,37},{7,38},{8,39},{9,... | collective-permute-start | bytes 24584
  725.9 16.1 %collective-permute-start.10 = (f32[24,256]{1,0:T(8,128)S(1)}, f32[24,256]{1,0:T(8,128)S(1)}, u32[]{:S(2)}, u32[]{:S(2)}) collective-permute-start(f32[24,256]{1,0:T(8,128)S(1)} %get-tuple-element.6), channel_id=1, source_target_pairs={{0,5},{1,6},{2,7},{3,8},{4,9},{5,10},{6,11},{7,12},{8,13},{9,14},{... | collective-permute-start | bytes 73736
  729.9 10.1 %collective-permute-start.37 = (f32[18,256]{1,0:T(8,128)S(1)}, f32[18,256]{1,0:T(8,128)S(1)}, u32[]{:S(2)}, u32[]{:S(2)}) collective-permute-start(f32[18,256]{1,0:T(8,128)S(1)} %slice.236), channel_id=1, source_target_pairs={{0,32},{1,33},{2,34},{3,35},{4,36},{5,37},{6,38},{7,39},{8,40},{9,... | collective-permute-start | bytes 55304
  731.9 14.6 %collective-permute-start.11 = (f32[24,256]{1,0:T(8,128)S(1)}, f32[24,256]{1,0:T(8,128)S(1)}, u32[]{:S(2)}, u32[]{:S(2)}) collective-permute-start(f32[24,256]{1,0:T(8,128)S(1)} %get-tuple-element.6), channel_id=1, source_target_pairs={{0,6},{1,7},{2,8},{3,9},{4,10},{5,11},{6,12},{7,13},{8,14},{9,15},... | collective-permute-start | bytes 73736
  733.7 14.8 %collective-permute-start.12 = (f32[24,256]{1,0:T(8,128)S(1)}, f32[24,256]{1,0:T(8,128)S(1)}, u32[]{:S(2)}, u32[]{:S(2)}) collective-permute-start(f32[24,256]{1,0:T(8,128)S(1)} %get-tuple-element.6), channel_id=1, source_target_pairs={{0,7},{1,8},{2,9},{3,10},{4,11},{5,12},{6,13},{7,14},{8,15},{9,16}... | collective-permute-start | bytes 73736
  735.9 15.5 %collective-permute-start.13 = (f32[24,256]{1,0:T(8,128)S(1)}, f32[24,256]{1,0:T(8,128)S(1)}, u32[]{:S(2)}, u32[]{:S(2)}) collective-permute-start(f32[24,256]{1,0:T(8,128)S(1)} %get-tuple-element.6), channel_id=1, source_target_pairs={{0,8},{1,9},{2,10},{3,11},{4,12},{5,13},{6,14},{7,15},{8,16},{9,17... | collective-permute-start | bytes 73736
  740.0 14.1 %collective-permute-start.14 = (f32[24,256]{1,0:T(8,128)S(1)}, f32[24,256]{1,0:T(8,128)S(1)}, u32[]{:S(2)}, u32[]{:S(2)}) collective-permute-start(f32[24,256]{1,0:T(8,128)S(1)} %get-tuple-element.6), channel_id=1, source_target_pairs={{0,9},{1,10},{2,11},{3,12},{4,13},{5,14},{6,15},{7,16},{8,17},{9,1... | collective-permute-start | bytes 73736
  742.0 16.1 %collective-permute-start.15 = (f32[24,256]{1,0:T(8,128)S(1)}, f32[24,256]{1,0:T(8,128)S(1)}, u32[]{:S(2)}, u32[]{:S(2)}) collective-permute-start(f32[24,256]{1,0:T(8,128)S(1)} %get-tuple-element.6), channel_id=1, source_target_pairs={{0,10},{1,11},{2,12},{3,13},{4,14},{5,15},{6,16},{7,17},{8,18},{9,... | collective-permute-start | bytes 73736
  746.5 15.6 %collective-permute-start.16 = (f32[24,256]{1,0:T(8,128)S(1)}, f32[24,256]{1,0:T(8,128)S(1)}, u32[]{:S(2)}, u32[]{:S(2)}) collective-permute-start(f32[24,256]{1,0:T(8,128)S(1)} %get-tuple-element.6), channel_id=1, source_target_pairs={{0,11},{1,12},{2,13},{3,14},{4,15},{5,16},{6,17},{7,18},{8,19},{9,... | collective-permute-start | bytes 73736
  748.5 14.9 %collective-permute-start.17 = (f32[24,256]{1,0:T(8,128)S(1)}, f32[24,256]{1,0:T(8,128)S(1)}, u32[]{:S(2)}, u32[]{:S(2)}) collective-permute-start(f32[24,256]{1,0:T(8,128)S(1)} %get-tuple-element.6), channel_id=1, source_target_pairs={{0,12},{1,13},{2,14},{3,15},{4,16},{5,17},{6,18},{7,19},{8,20},{9,... | collective-permute-start | bytes 73736
  751.4 13.3 %collective-permute-start.18 = (f32[24,256]{1,0:T(8,128)S(1)}, f32[24,256]{1,0:T(8,128)S(1)}, u32[]{:S(2)}, u32[]{:S(2)}) collective-permute-start(f32[24,256]{1,0:T(8,128)S(1)} %get-tuple-element.6), channel_id=1, source_target_pairs={{0,13},{1,14},{2,15},{3,16},{4,17},{5,18},{6,19},{7,20},{8,21},{9,... | collective-permute-start | bytes 73736
  754.2 13.2 %collective-permute-start.19 = (f32[24,256]{1,0:T(8,128)S(1)}, f32[24,256]{1,0:T(8,128)S(1)}, u32[]{:S(2)}, u32[]{:S(2)}) collective-permute-start(f32[24,256]{1,0:T(8,128)S(1)} %get-tuple-element.6), channel_id=1, source_target_pairs={{0,14},{1,15},{2,16},{3,17},{4,18},{5,19},{6,20},{7,21},{8,22},{9,... | collective-permute-start | bytes 73736
  758.1 12.8 %collective-permute-start.20 = (f32[24,256]{1,0:T(8,128)S(1)}, f32[24,256]{1,0:T(8,128)S(1)}, u32[]{:S(2)}, u32[]{:S(2)}) collective-permute-start(f32[24,256]{1,0:T(8,128)S(1)} %get-tuple-element.6), channel_id=1, source_target_pairs={{0,15},{1,16},{2,17},{3,18},{4,19},{5,20},{6,21},{7,22},{8,23},{9,... | collective-permute-start | bytes 73736
  762.1 10.5 %collective-permute-start.21 = (f32[24,256]{1,0:T(8,128)S(1)}, f32[24,256]{1,0:T(8,128)S(1)}, u32[]{:S(2)}, u32[]{:S(2)}) collective-permute-start(f32[24,256]{1,0:T(8,128)S(1)} %get-tuple-element.6), channel_id=1, source_target_pairs={{0,16},{1,17},{2,18},{3,19},{4,20},{5,21},{6,22},{7,23},{8,24},{9,... | collective-permute-start | bytes 73736
  763.5 11.2 %collective-permute-start.22 = (f32[24,256]{1,0:T(8,128)S(1)}, f32[24,256]{1,0:T(8,128)S(1)}, u32[]{:S(2)}, u32[]{:S(2)}) collective-permute-start(f32[24,256]{1,0:T(8,128)S(1)} %get-tuple-element.6), channel_id=1, source_target_pairs={{0,17},{1,18},{2,19},{3,20},{4,21},{5,22},{6,23},{7,24},{8,25},{9,... | collective-permute-start | bytes 73736
  764.8 11.9 %collective-permute-start.23 = (f32[24,256]{1,0:T(8,128)S(1)}, f32[24,256]{1,0:T(8,128)S(1)}, u32[]{:S(2)}, u32[]{:S(2)}) collective-permute-start(f32[24,256]{1,0:T(8,128)S(1)} %get-tuple-element.6), channel_id=1, source_target_pairs={{0,18},{1,19},{2,20},{3,21},{4,22},{5,23},{6,24},{7,25},{8,26},{9,... | collective-permute-start | bytes 73736
  767.4 10.7 %collective-permute-start.24 = (f32[24,256]{1,0:T(8,128)S(1)}, f32[24,256]{1,0:T(8,128)S(1)}, u32[]{:S(2)}, u32[]{:S(2)}) collective-permute-start(f32[24,256]{1,0:T(8,128)S(1)} %get-tuple-element.6), channel_id=1, source_target_pairs={{0,19},{1,20},{2,21},{3,22},{4,23},{5,24},{6,25},{7,26},{8,27},{9,... | collective-permute-start | bytes 73736
  772.7 13.1 %collective-permute-start.26 = (f32[24,256]{1,0:T(8,128)S(1)}, f32[24,256]{1,0:T(8,128)S(1)}, u32[]{:S(2)}, u32[]{:S(2)}) collective-permute-start(f32[24,256]{1,0:T(8,128)S(1)} %get-tuple-element.6), channel_id=1, source_target_pairs={{0,21},{1,22},{2,23},{3,24},{4,25},{5,26},{6,27},{7,28},{8,29},{9,... | collective-permute-start | bytes 73736
  774.6 13.9 %collective-permute-start.27 = (f32[24,256]{1,0:T(8,128)S(1)}, f32[24,256]{1,0:T(8,128)S(1)}, u32[]{:S(2)}, u32[]{:S(2)}) collective-permute-start(f32[24,256]{1,0:T(8,128)S(1)} %get-tuple-element.6), channel_id=1, source_target_pairs={{0,22},{1,23},{2,24},{3,25},{4,26},{5,27},{6,28},{7,29},{8,30},{9,... | collective-permute-start | bytes 73736
  776.7 13.6 %collective-permute-start.28 = (f32[24,256]{1,0:T(8,128)S(1)}, f32[24,256]{1,0:T(8,128)S(1)}, u32[]{:S(2)}, u32[]{:S(2)}) collective-permute-start(f32[24,256]{1,0:T(8,128)S(1)} %get-tuple-element.6), channel_id=1, source_target_pairs={{0,23},{1,24},{2,25},{3,26},{4,27},{5,28},{6,29},{7,30},{8,31},{9,... | collective-permute-start | bytes 73736
  778.1 14.2 %collective-permute-start.29 = (f32[24,256]{1,0:T(8,128)S(1)}, f32[24,256]{1,0:T(8,128)S(1)}, u32[]{:S(2)}, u32[]{:S(2)}) collective-permute-start(f32[24,256]{1,0:T(8,128)S(1)} %get-tuple-element.6), channel_id=1, source_target_pairs={{0,24},{1,25},{2,26},{3,27},{4,28},{5,29},{6,30},{7,31},{8,32},{9,... | collective-permute-start | bytes 73736
  780.4 13.1 %collective-permute-start.30 = (f32[24,256]{1,0:T(8,128)S(1)}, f32[24,256]{1,0:T(8,128)S(1)}, u32[]{:S(2)}, u32[]{:S(2)}) collective-permute-start(f32[24,256]{1,0:T(8,128)S(1)} %get-tuple-element.6), channel_id=1, source_target_pairs={{0,25},{1,26},{2,27},{3,28},{4,29},{5,30},{6,31},{7,32},{8,33},{9,... | collective-permute-start | bytes 73736
  785.8 17.4 %collective-permute-start.31 = (f32[24,256]{1,0:T(8,128)S(1)}, f32[24,256]{1,0:T(8,128)S(1)}, u32[]{:S(2)}, u32[]{:S(2)}) collective-permute-start(f32[24,256]{1,0:T(8,128)S(1)} %get-tuple-element.6), channel_id=1, source_target_pairs={{0,26},{1,27},{2,28},{3,29},{4,30},{5,31},{6,32},{7,33},{8,34},{9,... | collective-permute-start | bytes 73736
  788.6 15.9 %collective-permute-start.32 = (f32[24,256]{1,0:T(8,128)S(1)}, f32[24,256]{1,0:T(8,128)S(1)}, u32[]{:S(2)}, u32[]{:S(2)}) collective-permute-start(f32[24,256]{1,0:T(8,128)S(1)} %get-tuple-element.6), channel_id=1, source_target_pairs={{0,27},{1,28},{2,29},{3,30},{4,31},{5,32},{6,33},{7,34},{8,35},{9,... | collective-permute-start | bytes 73736
  790.2 16.2 %collective-permute-start.33 = (f32[24,256]{1,0:T(8,128)S(1)}, f32[24,256]{1,0:T(8,128)S(1)}, u32[]{:S(2)}, u32[]{:S(2)}) collective-permute-start(f32[24,256]{1,0:T(8,128)S(1)} %get-tuple-element.6), channel_id=1, source_target_pairs={{0,28},{1,29},{2,30},{3,31},{4,32},{5,33},{6,34},{7,35},{8,36},{9,... | collective-permute-start | bytes 73736
  792.2 17.0 %collective-permute-start.34 = (f32[24,256]{1,0:T(8,128)S(1)}, f32[24,256]{1,0:T(8,128)S(1)}, u32[]{:S(2)}, u32[]{:S(2)}) collective-permute-start(f32[24,256]{1,0:T(8,128)S(1)} %get-tuple-element.6), channel_id=1, source_target_pairs={{0,29},{1,30},{2,31},{3,32},{4,33},{5,34},{6,35},{7,36},{8,37},{9,... | collective-permute-start | bytes 73736
  793.6 20.1 %collective-permute-start.35 = (f32[24,256]{1,0:T(8,128)S(1)}, f32[24,256]{1,0:T(8,128)S(1)}, u32[]{:S(2)}, u32[]{:S(2)}) collective-permute-start(f32[24,256]{1,0:T(8,128)S(1)} %get-tuple-element.6), channel_id=1, source_target_pairs={{0,30},{1,31},{2,32},{3,33},{4,34},{5,35},{6,36},{7,37},{8,38},{9,... | collective-permute-start | bytes 73736
  803.2 13.0 %collective-permute-start.36 = (f32[24,256]{1,0:T(8,128)S(1)}, f32[24,256]{1,0:T(8,128)S(1)}, u32[]{:S(2)}, u32[]{:S(2)}) collective-permute-start(f32[24,256]{1,0:T(8,128)S(1)} %get-tuple-element.6), channel_id=1, source_target_pairs={{0,31},{1,32},{2,33},{3,34},{4,35},{5,36},{6,37},{7,38},{8,39},{9,... | collective-permute-start | bytes 73736
  804.5 11.7 %collective-permute-start.6 = (f32[24,256]{1,0:T(8,128)S(1)}, f32[24,256]{1,0:T(8,128)S(1)}, u32[]{:S(2)}, u32[]{:S(2)}) collective-permute-start(f32[24,256]{1,0:T(8,128)S(1)} %get-tuple-element.6), channel_id=1, source_target_pairs={{0,1},{1,2},{2,3},{3,4},{4,5},{5,6},{6,7},{7,8},{8,9},{9,10},{10,1... | collective-permute-start | bytes 73736
  806.5 9.8 %collective-permute-start.7 = (f32[24,256]{1,0:T(8,128)S(1)}, f32[24,256]{1,0:T(8,128)S(1)}, u32[]{:S(2)}, u32[]{:S(2)}) collective-permute-start(f32[24,256]{1,0:T(8,128)S(1)} %get-tuple-element.6), channel_id=1, source_target_pairs={{0,2},{1,3},{2,4},{3,5},{4,6},{5,7},{6,8},{7,9},{8,10},{9,11},{10,... | collective-permute-start | bytes 73736
  (81 other events, 908.4 us)
Sparse Core Ops, SparseCore 0:
  9.7 211.8 all-gather.3
where the time goes:
time: 839 us; the launch traced here: 833 us
  blocking collectives  504 us (60%)
  starting transfers between devices  179 us (21%)
  local copies, waits for them, and re-layouts  46.3 us (6%)
  matrix products  41.9 us (5%)
  other arithmetic  23.1 us (3%)
  waiting for transfers between devices  22.6 us (3%)
  between operations  16.5 us (2%)
    unnamed x1, blocking collectives  328 us
    all_gather x1, blocking collectives, shards(): lax.all_gather(temporal_weight, ('tm', 'rows'), axis=0, tiled=True)  176 us
    unnamed x64, starting transfers between devices  160 us
    dot_general x18, matrix products, conv_three(): jnp.dot(shifted_view(padded, tap_row, tap_col, n_rows, n_cols), block, pr...  21.6 us
    unnamed x155, local copies, waits for them, and re-layouts  21.2 us
  transfers between devices with their start and end apart: 71, of which 4 were waited for; matrix products, arithmetic and copies ran while one was open for 9% of the time, Pallas kernels for 0%

commit v1 on v0

--- a/solution.py
+++ b/solution.py
@@ -93,7 +93,12 @@
     n_batch, n_frames, n_rows, n_cols, chans = video.shape
     full_spatial, full_temporal = (
         lax.all_gather(spatial_weight, ("tm", "rows"), axis=0, tiled=True),
-        lax.all_gather(temporal_weight, ("tm", "rows"), axis=0, tiled=True),
+        jnp.concatenate(
+            lax.all_to_all(
+                jnp.stack([temporal_weight] * lax.axis_size(("tm", "rows"))), ("tm", "rows"), 0, 0
+            ),
+            axis=0,
+        ),
     )
     values = video.astype(jnp.float32)
     inv_rms = lax.rsqrt(jnp.mean(values * values, axis=-1, keepdims=True) + epsilon)

time: 839 us -> 839 us (level)
  blocking collectives: 504 us -> 322 us
  waiting for transfers between devices: 22.6 us -> 178 us
  starting transfers between devices: 179 us -> 202 us
    all_gather x1 -> x0, blocking collectives: 176 us -> none  [shards(): lax.all_gather(temporal_weight, ('tm', 'rows'), axis=0, tiled=True)]
    all_gather x1, waiting for transfers between devices: 8.46 us -> 154 us  [shards(): lax.all_gather(spatial_weight, ('tm', 'rows'), axis=0, tiled=True)]
    all_to_all x0 -> x1, starting transfers between devices: none -> 13 us  [shards(): lax.all_to_all(jnp.stack([temporal_weight] * lax.axis_size(('tm', 'rows')...]
    all_to_all x0 -> x1, waiting for transfers between devices: none -> 10.6 us  [shards(): lax.all_to_all(jnp.stack([temporal_weight] * lax.axis_size(('tm', 'rows')...]
    ppermute x2, starting transfers between devices: 7.99 us -> 17.6 us  [passed_along(): return lax.ppermute(x, axis, pairs)]
    unnamed x155 -> x154, local copies, waits for them, and re-layouts: 21.2 us -> 21.7 us
  transfers between devices with their start and end apart: 71 -> 72, of which waited for: 4 -> 5; matrix products, arithmetic and copies ran while one was open for 9% -> 10% of each run, Pallas kernels for 0% -> 0%
where the time goes in v1:
time: 839 us; the launch traced here: 833 us
  blocking collectives  322 us (38%)
  starting transfers between devices  202 us (24%)
  waiting for transfers between devices  178 us (21%)
  local copies, waits for them, and re-layouts  51.6 us (6%)
  matrix products  41.3 us (5%)
  other arithmetic  22.8 us (3%)
  between operations  16.5 us (2%)
    unnamed x1, blocking collectives  322 us
    unnamed x64, starting transfers between devices  160 us
    all_gather x1, waiting for transfers between devices, shards(): lax.all_gather(spatial_weight, ('tm', 'rows'), axis=0, tiled=True)  154 us
    unnamed x154, local copies, waits for them, and re-layouts  21.7 us
    dot_general x18, matrix products, conv_three(): jnp.dot(shifted_view(padded, tap_row, tap_col, n_rows, n_cols), block, pr...  21.6 us
    ppermute x2, starting transfers between devices, passed_along(): return lax.ppermute(x, axis, pairs)  17.6 us
  transfers between devices with their start and end apart: 72, of which 5 were waited for; matrix products, arithmetic and copies ran while one was open for 10% of the time, Pallas kernels for 0%

profile of v1, /device:TPU:4, one launch (start us, length us, event | category | flops | bytes accessed | tf_op | source)
XLA Modules:
  0.0 833.3 jit_solution(12150884721047331720)
XLA Ops:
  7.9 2.4 fusion.32
  14.3 3.6 collective-permute-start.1
  21.2 13.0 %all-to-all-start = ((bf16[128,6,256]{2,1,0:T(8,128)(2,1)}), bf16[128,6,256]{2,1,0:T(8,128)(2,1)S(1)}, u32[]{:S(2)}, u32[]{:S(2)}) async-start(bf16[128,6,256]{2,1,0:T(8,128)(2,1)} %stack.2), calls=%async_computation | async-start | bytes 1048576 | tf_op jit(solution)/shard_map/all_to_all | solution.py:97
  34.2 3.1 constant_dynamic-update-slice_fusion.1
  38.7 5.4 fusion.149
  44.2 2.3 pad_maximum_fusion.3
  46.4 10.6 %all-to-all-done = bf16[128,6,256]{2,1,0:T(8,128)(2,1)S(1)} async-done(((bf16[128,6,256]{2,1,0:T(8,128)(2,1)}), bf16[128,6,256]{2,1,0:T(8,128)(2,1)S(1)}, u32[]{:S(2)}, u32[]{:S(2)}) %all-to-all-start) | async-done | bytes 393248 | tf_op jit(solution)/shard_map/all_to_all | solution.py:97
  59.0 2.3 constant_dynamic-update-slice_fusion
  61.3 4.9 fusion.147
  66.2 153.5 %all-gather.3.cloned.1.call-done = bf16[128,18,256]{2,1,0:T(8,128)(2,1)} async-done(((bf16[1,18,256]{2,1,0:T(8,128)(2,1)}), bf16[128,18,256]{2,1,0:T(8,128)(2,1)}) %all-gather.3.cloned.1.call-update) | async-done | bytes 1179664 | tf_op jit(solution)/shard_map/all_gather | solution.py:95
  219.7 2.3 reshape.274
  222.0 2.4 fusion.135
  234.8 2.7 multiply_convert_fusion.1
  239.7 16.3 %collective-permute-start.2 = (bf16[1,2,8,128,256]{4,3,2,1,0:T(8,128)(2,1)}, bf16[1,2,8,128,256]{4,3,2,1,0:T(8,128)(2,1)}, u32[]{:S(2)}, u32[]{:S(2)}) collective-permute-start(bf16[1,2,8,128,256]{4,3,2,1,0:T(8,128)(2,1)} %slice.214), channel_id=1, source_target_pairs={{0,16},{16,32},{32,48},{48,64},{64,80},{80,96},{96,112},{1,17},{17... | collective-permute-start | bytes 3145736 | tf_op jit(solution)/shard_map/ppermute | solution.py:25
  256.1 2.7 multiply_convert_fusion
  270.0 3.6 collective-permute-start.5
  273.6 3.2 reshape.251
  279.7 3.1 fusion.111
  282.8 2.3 select_maximum_fusion
  285.1 3.2 pad_maximum_fusion.1
  288.3 4.6 fusion.148
  292.9 2.7 fusion.124
  298.5 3.8 fusion.57
  302.3 321.5 %fusion.146 = (f32[24,256]{1,0:T(8,128)S(1)}, f32[8,256]{1,0:T(8,128)S(1)}) fusion(f32[2304,256]{1,0:T(8,128)} %fusion.111, f32[768,256]{1,0:T(8,128)} %fusion.57), kind=kCustom, calls=%all-reduce-scatter.2 | all-reduce-scatter fusion | flops 1048578 | bytes 3178496
  623.8 1.9 collective-permute-start.38
  625.8 1.9 collective-permute-start.39
  627.7 1.9 collective-permute-start.40
  630.9 3.7 convolution_add_fusion.6
  634.6 1.9 collective-permute-start.41
  642.9 8.1 collective-permute-done.41
  651.0 10.5 %collective-permute-start.46 = (f32[8,256]{1,0:T(8,128)S(1)}, f32[8,256]{1,0:T(8,128)S(1)}, u32[]{:S(2)}, u32[]{:S(2)}) collective-permute-start(f32[8,256]{1,0:T(8,128)S(1)} %get-tuple-element.7), channel_id=1, source_target_pairs={{0,9},{1,10},{2,11},{3,12},{4,13},{5,14},{6,15},{7,16},{8,17},{9,1... | collective-permute-start | bytes 24584
  661.5 3.1 collective-permute-start.47
  667.6 18.5 %collective-permute-start.50 = (f32[8,256]{1,0:T(8,128)S(1)}, f32[8,256]{1,0:T(8,128)S(1)}, u32[]{:S(2)}, u32[]{:S(2)}) collective-permute-start(f32[8,256]{1,0:T(8,128)S(1)} %get-tuple-element.7), channel_id=1, source_target_pairs={{0,13},{1,14},{2,15},{3,16},{4,17},{5,18},{6,19},{7,20},{8,21},{9,... | collective-permute-start | bytes 24584
  686.9 2.9 collective-permute-start.51
  695.5 3.1 collective-permute-start.55
  699.5 3.8 collective-permute-start.56
  710.4 2.2 collective-permute-start.61
  714.3 2.8 collective-permute-start.63
  718.8 2.4 collective-permute-start.65
  726.3 4.0 collective-permute-start.10
  734.1 2.1 collective-permute-start.12
  736.2 4.2 collective-permute-start.13
  740.4 2.0 collective-permute-start.14
  742.4 3.7 collective-permute-start.15
  746.9 2.0 collective-permute-start.16
  748.9 2.9 collective-permute-start.17
  751.8 2.7 collective-permute-start.18
  754.6 3.9 collective-permute-start.19
  760.1 2.4 fusion.27
  765.1 2.6 collective-permute-start.23
  767.8 3.5 collective-permute-start.24
  773.0 2.0 collective-permute-start.26
  775.0 2.0 collective-permute-start.27
  778.5 2.3 collective-permute-start.29
  782.5 3.7 fusion.31
  786.2 2.8 collective-permute-start.31
  790.6 2.0 collective-permute-start.33
  793.9 2.3 collective-permute-start.35
  796.4 4.1 fusion.33
  800.7 2.9 concatenate.53
  806.9 2.7 collective-permute-start.7
  809.6 4.5 collective-permute-start.8
  816.7 4.7 collective-permute-done.9
  821.3 4.3 concatenate.52
  (296 shorter events, 96.5 us)
Async XLA Ops:
  7.2 212.5 %all-gather.3.cloned.1.call-start = ((), (), s32[]{:S(2)}) async-start(), calls=%async_computation.1 | async-start | bytes 1585152 | tf_op jit(solution)/shard_map/all_gather | solution.py:95
  12.4 25.0 %collective-permute-start = (bf16[1,4,1,128,256]{4,3,2,1,0:T(8,128)(2,1)}, bf16[1,4,1,128,256]{4,3,2,1,0:T(8,128)(2,1)S(1)}, u32[]{:S(2)}, u32[]{:S(2)}) collective-permute-start(bf16[1,4,1,128,256]{4,3,2,1,0:T(8,128)(2,1)} %get-tuple-element.28), channel_id=1, source_target_pairs={{0,1},{1,2},{2,3},{3,4},{4,5},{5,6},{6,7},{7,8},{8,9},{9,10},{10,1... | collective-permute-start | bytes 786440 | tf_op jit(solution)/shard_map/ppermute | solution.py:16
  14.3 23.1 %collective-permute-start.1 = (bf16[1,4,1,128,256]{4,3,2,1,0:T(8,128)(2,1)S(1)}, bf16[1,4,1,128,256]{4,3,2,1,0:T(8,128)(2,1)S(1)}, u32[]{:S(2)}, u32[]{:S(2)}) collective-permute-start(bf16[1,4,1,128,256]{4,3,2,1,0:T(8,128)(2,1)S(1)} %get-tuple-element.29), channel_id=1, source_target_pairs={{1,0},{2,1},{3,2},{4,3},{5,4},{6,5},{7,6},{8,7},{9,8},{10,9},{11,1... | collective-permute-start | bytes 786440 | tf_op jit(solution)/shard_map/ppermute | solution.py:17
  19.1 39.9 %collective-permute-start.3 = (bf16[1,2,8,128,256]{4,3,2,1,0:T(8,128)(2,1)}, bf16[1,2,8,128,256]{4,3,2,1,0:T(8,128)(2,1)}, u32[]{:S(2)}, u32[]{:S(2)}) collective-permute-start(bf16[1,2,8,128,256]{4,3,2,1,0:T(8,128)(2,1)} %slice.175), channel_id=1, source_target_pairs={{16,0},{32,16},{48,32},{64,48},{80,64},{96,80},{112,96},{17,1},{33... | collective-permute-start | bytes 3145736 | tf_op jit(solution)/shard_map/ppermute | solution.py:25
  21.2 35.8 %all-to-all-start = ((bf16[128,6,256]{2,1,0:T(8,128)(2,1)}), bf16[128,6,256]{2,1,0:T(8,128)(2,1)S(1)}, u32[]{:S(2)}, u32[]{:S(2)}) async-start(bf16[128,6,256]{2,1,0:T(8,128)(2,1)} %stack.2), calls=%async_computation | async-start | bytes 1048576 | tf_op jit(solution)/shard_map/all_to_all | solution.py:97
  239.7 55.9 %collective-permute-start.2 = (bf16[1,2,8,128,256]{4,3,2,1,0:T(8,128)(2,1)}, bf16[1,2,8,128,256]{4,3,2,1,0:T(8,128)(2,1)}, u32[]{:S(2)}, u32[]{:S(2)}) collective-permute-start(bf16[1,2,8,128,256]{4,3,2,1,0:T(8,128)(2,1)} %slice.214), channel_id=1, source_target_pairs={{0,16},{16,32},{32,48},{48,64},{64,80},{80,96},{96,112},{1,17},{17... | collective-permute-start | bytes 3145736 | tf_op jit(solution)/shard_map/ppermute | solution.py:25
  268.0 14.7 %collective-permute-start.4 = (bf16[1,4,1,128,256]{4,3,2,1,0:T(8,128)(2,1)}, bf16[1,4,1,128,256]{4,3,2,1,0:T(8,128)(2,1)S(1)}, u32[]{:S(2)}, u32[]{:S(2)}) collective-permute-start(bf16[1,4,1,128,256]{4,3,2,1,0:T(8,128)(2,1)} %get-tuple-element.24), channel_id=1, source_target_pairs={{0,1},{1,2},{2,3},{3,4},{4,5},{5,6},{6,7},{7,8},{8,9},{9,10},{10,1... | collective-permute-start | bytes 786440 | tf_op jit(solution)/shard_map/ppermute | solution.py:16
  270.0 12.8 %collective-permute-start.5 = (bf16[1,4,1,128,256]{4,3,2,1,0:T(8,128)(2,1)}, bf16[1,4,1,128,256]{4,3,2,1,0:T(8,128)(2,1)}, u32[]{:S(2)}, u32[]{:S(2)}) collective-permute-start(bf16[1,4,1,128,256]{4,3,2,1,0:T(8,128)(2,1)} %get-tuple-element.25), channel_id=1, source_target_pairs={{1,0},{2,1},{3,2},{4,3},{5,4},{6,5},{7,6},{8,7},{9,8},{10,9},{11,1... | collective-permute-start | bytes 786440 | tf_op jit(solution)/shard_map/ppermute | solution.py:17
  623.8 14.0 %collective-permute-start.38 = (f32[8,256]{1,0:T(8,128)S(1)}, f32[8,256]{1,0:T(8,128)S(1)}, u32[]{:S(2)}, u32[]{:S(2)}) collective-permute-start(f32[8,256]{1,0:T(8,128)S(1)} %get-tuple-element.7), channel_id=1, source_target_pairs={{0,1},{1,2},{2,3},{3,4},{4,5},{5,6},{6,7},{7,8},{8,9},{9,10},{10,1... | collective-permute-start | bytes 24584
  625.8 13.4 %collective-permute-start.39 = (f32[8,256]{1,0:T(8,128)S(1)}, f32[8,256]{1,0:T(8,128)S(1)}, u32[]{:S(2)}, u32[]{:S(2)}) collective-permute-start(f32[8,256]{1,0:T(8,128)S(1)} %get-tuple-element.7), channel_id=1, source_target_pairs={{0,2},{1,3},{2,4},{3,5},{4,6},{5,7},{6,8},{7,9},{8,10},{9,11},{10,... | collective-permute-start | bytes 24584
  627.7 13.1 %collective-permute-start.40 = (f32[8,256]{1,0:T(8,128)S(1)}, f32[8,256]{1,0:T(8,128)S(1)}, u32[]{:S(2)}, u32[]{:S(2)}) collective-permute-start(f32[8,256]{1,0:T(8,128)S(1)} %get-tuple-element.7), channel_id=1, source_target_pairs={{0,3},{1,4},{2,5},{3,6},{4,7},{5,8},{6,9},{7,10},{8,11},{9,12},{10... | collective-permute-start | bytes 24584
  634.6 16.4 %collective-permute-start.41 = (f32[8,256]{1,0:T(8,128)S(1)}, f32[8,256]{1,0:T(8,128)S(1)}, u32[]{:S(2)}, u32[]{:S(2)}) collective-permute-start(f32[8,256]{1,0:T(8,128)S(1)} %get-tuple-element.7), channel_id=1, source_target_pairs={{0,4},{1,5},{2,6},{3,7},{4,8},{5,9},{6,10},{7,11},{8,12},{9,13},{1... | collective-permute-start | bytes 24584
  636.6 24.9 %collective-permute-start.42 = (f32[8,256]{1,0:T(8,128)S(1)}, f32[8,256]{1,0:T(8,128)S(1)}, u32[]{:S(2)}, u32[]{:S(2)}) collective-permute-start(f32[8,256]{1,0:T(8,128)S(1)} %get-tuple-element.7), channel_id=1, source_target_pairs={{0,5},{1,6},{2,7},{3,8},{4,9},{5,10},{6,11},{7,12},{8,13},{9,14},{... | collective-permute-start | bytes 24584
  637.9 26.7 %collective-permute-start.43 = (f32[8,256]{1,0:T(8,128)S(1)}, f32[8,256]{1,0:T(8,128)S(1)}, u32[]{:S(2)}, u32[]{:S(2)}) collective-permute-start(f32[8,256]{1,0:T(8,128)S(1)} %get-tuple-element.7), channel_id=1, source_target_pairs={{0,6},{1,7},{2,8},{3,9},{4,10},{5,11},{6,12},{7,13},{8,14},{9,15},... | collective-permute-start | bytes 24584
  639.2 26.7 %collective-permute-start.44 = (f32[8,256]{1,0:T(8,128)S(1)}, f32[8,256]{1,0:T(8,128)S(1)}, u32[]{:S(2)}, u32[]{:S(2)}) collective-permute-start(f32[8,256]{1,0:T(8,128)S(1)} %get-tuple-element.7), channel_id=1, source_target_pairs={{0,7},{1,8},{2,9},{3,10},{4,11},{5,12},{6,13},{7,14},{8,15},{9,16}... | collective-permute-start | bytes 24584
  640.8 26.7 %collective-permute-start.45 = (f32[8,256]{1,0:T(8,128)S(1)}, f32[8,256]{1,0:T(8,128)S(1)}, u32[]{:S(2)}, u32[]{:S(2)}) collective-permute-start(f32[8,256]{1,0:T(8,128)S(1)} %get-tuple-element.7), channel_id=1, source_target_pairs={{0,8},{1,9},{2,10},{3,11},{4,12},{5,13},{6,14},{7,15},{8,16},{9,17... | collective-permute-start | bytes 24584
  651.0 35.9 %collective-permute-start.46 = (f32[8,256]{1,0:T(8,128)S(1)}, f32[8,256]{1,0:T(8,128)S(1)}, u32[]{:S(2)}, u32[]{:S(2)}) collective-permute-start(f32[8,256]{1,0:T(8,128)S(1)} %get-tuple-element.7), channel_id=1, source_target_pairs={{0,9},{1,10},{2,11},{3,12},{4,13},{5,14},{6,15},{7,16},{8,17},{9,1... | collective-permute-start | bytes 24584
  661.5 28.3 %collective-permute-start.47 = (f32[8,256]{1,0:T(8,128)S(1)}, f32[8,256]{1,0:T(8,128)S(1)}, u32[]{:S(2)}, u32[]{:S(2)}) collective-permute-start(f32[8,256]{1,0:T(8,128)S(1)} %get-tuple-element.7), channel_id=1, source_target_pairs={{0,10},{1,11},{2,12},{3,13},{4,14},{5,15},{6,16},{7,17},{8,18},{9,... | collective-permute-start | bytes 24584
  664.6 27.2 %collective-permute-start.48 = (f32[8,256]{1,0:T(8,128)S(1)}, f32[8,256]{1,0:T(8,128)S(1)}, u32[]{:S(2)}, u32[]{:S(2)}) collective-permute-start(f32[8,256]{1,0:T(8,128)S(1)} %get-tuple-element.7), channel_id=1, source_target_pairs={{0,11},{1,12},{2,13},{3,14},{4,15},{5,16},{6,17},{7,18},{8,19},{9,... | collective-permute-start | bytes 24584
  665.9 27.7 %collective-permute-start.49 = (f32[8,256]{1,0:T(8,128)S(1)}, f32[8,256]{1,0:T(8,128)S(1)}, u32[]{:S(2)}, u32[]{:S(2)}) collective-permute-start(f32[8,256]{1,0:T(8,128)S(1)} %get-tuple-element.7), channel_id=1, source_target_pairs={{0,12},{1,13},{2,14},{3,15},{4,16},{5,17},{6,18},{7,19},{8,20},{9,... | collective-permute-start | bytes 24584
  667.6 27.9 %collective-permute-start.50 = (f32[8,256]{1,0:T(8,128)S(1)}, f32[8,256]{1,0:T(8,128)S(1)}, u32[]{:S(2)}, u32[]{:S(2)}) collective-permute-start(f32[8,256]{1,0:T(8,128)S(1)} %get-tuple-element.7), channel_id=1, source_target_pairs={{0,13},{1,14},{2,15},{3,16},{4,17},{5,18},{6,19},{7,20},{8,21},{9,... | collective-permute-start | bytes 24584
  686.9 12.6 %collective-permute-start.51 = (f32[8,256]{1,0:T(8,128)S(1)}, f32[8,256]{1,0:T(8,128)S(1)}, u32[]{:S(2)}, u32[]{:S(2)}) collective-permute-start(f32[8,256]{1,0:T(8,128)S(1)} %get-tuple-element.7), channel_id=1, source_target_pairs={{0,14},{1,15},{2,16},{3,17},{4,18},{5,19},{6,20},{7,21},{8,22},{9,... | collective-permute-start | bytes 24584
  689.8 13.5 %collective-permute-start.52 = (f32[8,256]{1,0:T(8,128)S(1)}, f32[8,256]{1,0:T(8,128)S(1)}, u32[]{:S(2)}, u32[]{:S(2)}) collective-permute-start(f32[8,256]{1,0:T(8,128)S(1)} %get-tuple-element.7), channel_id=1, source_target_pairs={{0,15},{1,16},{2,17},{3,18},{4,19},{5,20},{6,21},{7,22},{8,23},{9,... | collective-permute-start | bytes 24584
  691.8 13.2 %collective-permute-start.53 = (f32[8,256]{1,0:T(8,128)S(1)}, f32[8,256]{1,0:T(8,128)S(1)}, u32[]{:S(2)}, u32[]{:S(2)}) collective-permute-start(f32[8,256]{1,0:T(8,128)S(1)} %get-tuple-element.7), channel_id=1, source_target_pairs={{0,16},{1,17},{2,18},{3,19},{4,20},{5,21},{6,22},{7,23},{8,24},{9,... | collective-permute-start | bytes 24584
  693.6 13.0 %collective-permute-start.54 = (f32[8,256]{1,0:T(8,128)S(1)}, f32[8,256]{1,0:T(8,128)S(1)}, u32[]{:S(2)}, u32[]{:S(2)}) collective-permute-start(f32[8,256]{1,0:T(8,128)S(1)} %get-tuple-element.7), channel_id=1, source_target_pairs={{0,17},{1,18},{2,19},{3,20},{4,21},{5,22},{6,23},{7,24},{8,25},{9,... | collective-permute-start | bytes 24584
  695.5 12.4 %collective-permute-start.55 = (f32[8,256]{1,0:T(8,128)S(1)}, f32[8,256]{1,0:T(8,128)S(1)}, u32[]{:S(2)}, u32[]{:S(2)}) collective-permute-start(f32[8,256]{1,0:T(8,128)S(1)} %get-tuple-element.7), channel_id=1, source_target_pairs={{0,18},{1,19},{2,20},{3,21},{4,22},{5,23},{6,24},{7,25},{8,26},{9,... | collective-permute-start | bytes 24584
  699.5 10.9 %collective-permute-start.56 = (f32[8,256]{1,0:T(8,128)S(1)}, f32[8,256]{1,0:T(8,128)S(1)}, u32[]{:S(2)}, u32[]{:S(2)}) collective-permute-start(f32[8,256]{1,0:T(8,128)S(1)} %get-tuple-element.7), channel_id=1, source_target_pairs={{0,19},{1,20},{2,21},{3,22},{4,23},{5,24},{6,25},{7,26},{8,27},{9,... | collective-permute-start | bytes 24584
  706.6 10.5 %collective-permute-start.59 = (f32[8,256]{1,0:T(8,128)S(1)}, f32[8,256]{1,0:T(8,128)S(1)}, u32[]{:S(2)}, u32[]{:S(2)}) collective-permute-start(f32[8,256]{1,0:T(8,128)S(1)} %get-tuple-element.7), channel_id=1, source_target_pairs={{0,22},{1,23},{2,24},{3,25},{4,26},{5,27},{6,28},{7,29},{8,30},{9,... | collective-permute-start | bytes 24584
  708.0 10.8 %collective-permute-start.60 = (f32[8,256]{1,0:T(8,128)S(1)}, f32[8,256]{1,0:T(8,128)S(1)}, u32[]{:S(2)}, u32[]{:S(2)}) collective-permute-start(f32[8,256]{1,0:T(8,128)S(1)} %get-tuple-element.7), channel_id=1, source_target_pairs={{0,23},{1,24},{2,25},{3,26},{4,27},{5,28},{6,29},{7,30},{8,31},{9,... | collective-permute-start | bytes 24584
  710.4 11.5 %collective-permute-start.61 = (f32[8,256]{1,0:T(8,128)S(1)}, f32[8,256]{1,0:T(8,128)S(1)}, u32[]{:S(2)}, u32[]{:S(2)}) collective-permute-start(f32[8,256]{1,0:T(8,128)S(1)} %get-tuple-element.7), channel_id=1, source_target_pairs={{0,24},{1,25},{2,26},{3,27},{4,28},{5,29},{6,30},{7,31},{8,32},{9,... | collective-permute-start | bytes 24584
  712.7 10.9 %collective-permute-start.62 = (f32[8,256]{1,0:T(8,128)S(1)}, f32[8,256]{1,0:T(8,128)S(1)}, u32[]{:S(2)}, u32[]{:S(2)}) collective-permute-start(f32[8,256]{1,0:T(8,128)S(1)} %get-tuple-element.7), channel_id=1, source_target_pairs={{0,25},{1,26},{2,27},{3,28},{4,29},{5,30},{6,31},{7,32},{8,33},{9,... | collective-permute-start | bytes 24584
  714.3 10.6 %collective-permute-start.63 = (f32[8,256]{1,0:T(8,128)S(1)}, f32[8,256]{1,0:T(8,128)S(1)}, u32[]{:S(2)}, u32[]{:S(2)}) collective-permute-start(f32[8,256]{1,0:T(8,128)S(1)} %get-tuple-element.7), channel_id=1, source_target_pairs={{0,26},{1,27},{2,28},{3,29},{4,30},{5,31},{6,32},{7,33},{8,34},{9,... | collective-permute-start | bytes 24584
  718.8 11.5 %collective-permute-start.65 = (f32[8,256]{1,0:T(8,128)S(1)}, f32[8,256]{1,0:T(8,128)S(1)}, u32[]{:S(2)}, u32[]{:S(2)}) collective-permute-start(f32[8,256]{1,0:T(8,128)S(1)} %get-tuple-element.7), channel_id=1, source_target_pairs={{0,28},{1,29},{2,30},{3,31},{4,32},{5,33},{6,34},{7,35},{8,36},{9,... | collective-permute-start | bytes 24584
  721.9 10.4 %collective-permute-start.66 = (f32[8,256]{1,0:T(8,128)S(1)}, f32[8,256]{1,0:T(8,128)S(1)}, u32[]{:S(2)}, u32[]{:S(2)}) collective-permute-start(f32[8,256]{1,0:T(8,128)S(1)} %get-tuple-element.7), channel_id=1, source_target_pairs={{0,29},{1,30},{2,31},{3,32},{4,33},{5,34},{6,35},{7,36},{8,37},{9,... | collective-permute-start | bytes 24584
  723.6 10.5 %collective-permute-start.67 = (f32[8,256]{1,0:T(8,128)S(1)}, f32[8,256]{1,0:T(8,128)S(1)}, u32[]{:S(2)}, u32[]{:S(2)}) collective-permute-start(f32[8,256]{1,0:T(8,128)S(1)} %get-tuple-element.7), channel_id=1, source_target_pairs={{0,30},{1,31},{2,32},{3,33},{4,34},{5,35},{6,36},{7,37},{8,38},{9,... | collective-permute-start | bytes 24584
  724.9 11.3 %collective-permute-start.68 = (f32[8,256]{1,0:T(8,128)S(1)}, f32[8,256]{1,0:T(8,128)S(1)}, u32[]{:S(2)}, u32[]{:S(2)}) collective-permute-start(f32[8,256]{1,0:T(8,128)S(1)} %get-tuple-element.7), channel_id=1, source_target_pairs={{0,31},{1,32},{2,33},{3,34},{4,35},{5,36},{6,37},{7,38},{8,39},{9,... | collective-permute-start | bytes 24584
  726.3 16.1 %collective-permute-start.10 = (f32[24,256]{1,0:T(8,128)S(1)}, f32[24,256]{1,0:T(8,128)S(1)}, u32[]{:S(2)}, u32[]{:S(2)}) collective-permute-start(f32[24,256]{1,0:T(8,128)S(1)} %get-tuple-element.6), channel_id=1, source_target_pairs={{0,5},{1,6},{2,7},{3,8},{4,9},{5,10},{6,11},{7,12},{8,13},{9,14},{... | collective-permute-start | bytes 73736
  730.3 10.1 %collective-permute-start.37 = (f32[18,256]{1,0:T(8,128)S(1)}, f32[18,256]{1,0:T(8,128)S(1)}, u32[]{:S(2)}, u32[]{:S(2)}) collective-permute-start(f32[18,256]{1,0:T(8,128)S(1)} %slice.236), channel_id=1, source_target_pairs={{0,32},{1,33},{2,34},{3,35},{4,36},{5,37},{6,38},{7,39},{8,40},{9,... | collective-permute-start | bytes 55304
  732.3 14.6 %collective-permute-start.11 = (f32[24,256]{1,0:T(8,128)S(1)}, f32[24,256]{1,0:T(8,128)S(1)}, u32[]{:S(2)}, u32[]{:S(2)}) collective-permute-start(f32[24,256]{1,0:T(8,128)S(1)} %get-tuple-element.6), channel_id=1, source_target_pairs={{0,6},{1,7},{2,8},{3,9},{4,10},{5,11},{6,12},{7,13},{8,14},{9,15},... | collective-permute-start | bytes 73736
  734.1 14.8 %collective-permute-start.12 = (f32[24,256]{1,0:T(8,128)S(1)}, f32[24,256]{1,0:T(8,128)S(1)}, u32[]{:S(2)}, u32[]{:S(2)}) collective-permute-start(f32[24,256]{1,0:T(8,128)S(1)} %get-tuple-element.6), channel_id=1, source_target_pairs={{0,7},{1,8},{2,9},{3,10},{4,11},{5,12},{6,13},{7,14},{8,15},{9,16}... | collective-permute-start | bytes 73736
  736.2 15.6 %collective-permute-start.13 = (f32[24,256]{1,0:T(8,128)S(1)}, f32[24,256]{1,0:T(8,128)S(1)}, u32[]{:S(2)}, u32[]{:S(2)}) collective-permute-start(f32[24,256]{1,0:T(8,128)S(1)} %get-tuple-element.6), channel_id=1, source_target_pairs={{0,8},{1,9},{2,10},{3,11},{4,12},{5,13},{6,14},{7,15},{8,16},{9,17... | collective-permute-start | bytes 73736
  740.4 14.1 %collective-permute-start.14 = (f32[24,256]{1,0:T(8,128)S(1)}, f32[24,256]{1,0:T(8,128)S(1)}, u32[]{:S(2)}, u32[]{:S(2)}) collective-permute-start(f32[24,256]{1,0:T(8,128)S(1)} %get-tuple-element.6), channel_id=1, source_target_pairs={{0,9},{1,10},{2,11},{3,12},{4,13},{5,14},{6,15},{7,16},{8,17},{9,1... | collective-permute-start | bytes 73736
  742.4 16.1 %collective-permute-start.15 = (f32[24,256]{1,0:T(8,128)S(1)}, f32[24,256]{1,0:T(8,128)S(1)}, u32[]{:S(2)}, u32[]{:S(2)}) collective-permute-start(f32[24,256]{1,0:T(8,128)S(1)} %get-tuple-element.6), channel_id=1, source_target_pairs={{0,10},{1,11},{2,12},{3,13},{4,14},{5,15},{6,16},{7,17},{8,18},{9,... | collective-permute-start | bytes 73736
  746.9 15.6 %collective-permute-start.16 = (f32[24,256]{1,0:T(8,128)S(1)}, f32[24,256]{1,0:T(8,128)S(1)}, u32[]{:S(2)}, u32[]{:S(2)}) collective-permute-start(f32[24,256]{1,0:T(8,128)S(1)} %get-tuple-element.6), channel_id=1, source_target_pairs={{0,11},{1,12},{2,13},{3,14},{4,15},{5,16},{6,17},{7,18},{8,19},{9,... | collective-permute-start | bytes 73736
  748.9 14.9 %collective-permute-start.17 = (f32[24,256]{1,0:T(8,128)S(1)}, f32[24,256]{1,0:T(8,128)S(1)}, u32[]{:S(2)}, u32[]{:S(2)}) collective-permute-start(f32[24,256]{1,0:T(8,128)S(1)} %get-tuple-element.6), channel_id=1, source_target_pairs={{0,12},{1,13},{2,14},{3,15},{4,16},{5,17},{6,18},{7,19},{8,20},{9,... | collective-permute-start | bytes 73736
  751.8 13.3 %collective-permute-start.18 = (f32[24,256]{1,0:T(8,128)S(1)}, f32[24,256]{1,0:T(8,128)S(1)}, u32[]{:S(2)}, u32[]{:S(2)}) collective-permute-start(f32[24,256]{1,0:T(8,128)S(1)} %get-tuple-element.6), channel_id=1, source_target_pairs={{0,13},{1,14},{2,15},{3,16},{4,17},{5,18},{6,19},{7,20},{8,21},{9,... | collective-permute-start | bytes 73736
  754.6 13.2 %collective-permute-start.19 = (f32[24,256]{1,0:T(8,128)S(1)}, f32[24,256]{1,0:T(8,128)S(1)}, u32[]{:S(2)}, u32[]{:S(2)}) collective-permute-start(f32[24,256]{1,0:T(8,128)S(1)} %get-tuple-element.6), channel_id=1, source_target_pairs={{0,14},{1,15},{2,16},{3,17},{4,18},{5,19},{6,20},{7,21},{8,22},{9,... | collective-permute-start | bytes 73736
  758.5 12.8 %collective-permute-start.20 = (f32[24,256]{1,0:T(8,128)S(1)}, f32[24,256]{1,0:T(8,128)S(1)}, u32[]{:S(2)}, u32[]{:S(2)}) collective-permute-start(f32[24,256]{1,0:T(8,128)S(1)} %get-tuple-element.6), channel_id=1, source_target_pairs={{0,15},{1,16},{2,17},{3,18},{4,19},{5,20},{6,21},{7,22},{8,23},{9,... | collective-permute-start | bytes 73736
  762.5 10.5 %collective-permute-start.21 = (f32[24,256]{1,0:T(8,128)S(1)}, f32[24,256]{1,0:T(8,128)S(1)}, u32[]{:S(2)}, u32[]{:S(2)}) collective-permute-start(f32[24,256]{1,0:T(8,128)S(1)} %get-tuple-element.6), channel_id=1, source_target_pairs={{0,16},{1,17},{2,18},{3,19},{4,20},{5,21},{6,22},{7,23},{8,24},{9,... | collective-permute-start | bytes 73736
  763.8 11.2 %collective-permute-start.22 = (f32[24,256]{1,0:T(8,128)S(1)}, f32[24,256]{1,0:T(8,128)S(1)}, u32[]{:S(2)}, u32[]{:S(2)}) collective-permute-start(f32[24,256]{1,0:T(8,128)S(1)} %get-tuple-element.6), channel_id=1, source_target_pairs={{0,17},{1,18},{2,19},{3,20},{4,21},{5,22},{6,23},{7,24},{8,25},{9,... | collective-permute-start | bytes 73736
  765.1 11.9 %collective-permute-start.23 = (f32[24,256]{1,0:T(8,128)S(1)}, f32[24,256]{1,0:T(8,128)S(1)}, u32[]{:S(2)}, u32[]{:S(2)}) collective-permute-start(f32[24,256]{1,0:T(8,128)S(1)} %get-tuple-element.6), channel_id=1, source_target_pairs={{0,18},{1,19},{2,20},{3,21},{4,22},{5,23},{6,24},{7,25},{8,26},{9,... | collective-permute-start | bytes 73736
  767.8 10.7 %collective-permute-start.24 = (f32[24,256]{1,0:T(8,128)S(1)}, f32[24,256]{1,0:T(8,128)S(1)}, u32[]{:S(2)}, u32[]{:S(2)}) collective-permute-start(f32[24,256]{1,0:T(8,128)S(1)} %get-tuple-element.6), channel_id=1, source_target_pairs={{0,19},{1,20},{2,21},{3,22},{4,23},{5,24},{6,25},{7,26},{8,27},{9,... | collective-permute-start | bytes 73736
  773.0 13.1 %collective-permute-start.26 = (f32[24,256]{1,0:T(8,128)S(1)}, f32[24,256]{1,0:T(8,128)S(1)}, u32[]{:S(2)}, u32[]{:S(2)}) collective-permute-start(f32[24,256]{1,0:T(8,128)S(1)} %get-tuple-element.6), channel_id=1, source_target_pairs={{0,21},{1,22},{2,23},{3,24},{4,25},{5,26},{6,27},{7,28},{8,29},{9,... | collective-permute-start | bytes 73736
  775.0 14.0 %collective-permute-start.27 = (f32[24,256]{1,0:T(8,128)S(1)}, f32[24,256]{1,0:T(8,128)S(1)}, u32[]{:S(2)}, u32[]{:S(2)}) collective-permute-start(f32[24,256]{1,0:T(8,128)S(1)} %get-tuple-element.6), channel_id=1, source_target_pairs={{0,22},{1,23},{2,24},{3,25},{4,26},{5,27},{6,28},{7,29},{8,30},{9,... | collective-permute-start | bytes 73736
  777.0 13.6 %collective-permute-start.28 = (f32[24,256]{1,0:T(8,128)S(1)}, f32[24,256]{1,0:T(8,128)S(1)}, u32[]{:S(2)}, u32[]{:S(2)}) collective-permute-start(f32[24,256]{1,0:T(8,128)S(1)} %get-tuple-element.6), channel_id=1, source_target_pairs={{0,23},{1,24},{2,25},{3,26},{4,27},{5,28},{6,29},{7,30},{8,31},{9,... | collective-permute-start | bytes 73736
  778.5 14.2 %collective-permute-start.29 = (f32[24,256]{1,0:T(8,128)S(1)}, f32[24,256]{1,0:T(8,128)S(1)}, u32[]{:S(2)}, u32[]{:S(2)}) collective-permute-start(f32[24,256]{1,0:T(8,128)S(1)} %get-tuple-element.6), channel_id=1, source_target_pairs={{0,24},{1,25},{2,26},{3,27},{4,28},{5,29},{6,30},{7,31},{8,32},{9,... | collective-permute-start | bytes 73736
  780.8 13.1 %collective-permute-start.30 = (f32[24,256]{1,0:T(8,128)S(1)}, f32[24,256]{1,0:T(8,128)S(1)}, u32[]{:S(2)}, u32[]{:S(2)}) collective-permute-start(f32[24,256]{1,0:T(8,128)S(1)} %get-tuple-element.6), channel_id=1, source_target_pairs={{0,25},{1,26},{2,27},{3,28},{4,29},{5,30},{6,31},{7,32},{8,33},{9,... | collective-permute-start | bytes 73736
  786.2 17.4 %collective-permute-start.31 = (f32[24,256]{1,0:T(8,128)S(1)}, f32[24,256]{1,0:T(8,128)S(1)}, u32[]{:S(2)}, u32[]{:S(2)}) collective-permute-start(f32[24,256]{1,0:T(8,128)S(1)} %get-tuple-element.6), channel_id=1, source_target_pairs={{0,26},{1,27},{2,28},{3,29},{4,30},{5,31},{6,32},{7,33},{8,34},{9,... | collective-permute-start | bytes 73736
  789.0 15.9 %collective-permute-start.32 = (f32[24,256]{1,0:T(8,128)S(1)}, f32[24,256]{1,0:T(8,128)S(1)}, u32[]{:S(2)}, u32[]{:S(2)}) collective-permute-start(f32[24,256]{1,0:T(8,128)S(1)} %get-tuple-element.6), channel_id=1, source_target_pairs={{0,27},{1,28},{2,29},{3,30},{4,31},{5,32},{6,33},{7,34},{8,35},{9,... | collective-permute-start | bytes 73736
  790.6 16.2 %collective-permute-start.33 = (f32[24,256]{1,0:T(8,128)S(1)}, f32[24,256]{1,0:T(8,128)S(1)}, u32[]{:S(2)}, u32[]{:S(2)}) collective-permute-start(f32[24,256]{1,0:T(8,128)S(1)} %get-tuple-element.6), channel_id=1, source_target_pairs={{0,28},{1,29},{2,30},{3,31},{4,32},{5,33},{6,34},{7,35},{8,36},{9,... | collective-permute-start | bytes 73736
  792.6 17.0 %collective-permute-start.34 = (f32[24,256]{1,0:T(8,128)S(1)}, f32[24,256]{1,0:T(8,128)S(1)}, u32[]{:S(2)}, u32[]{:S(2)}) collective-permute-start(f32[24,256]{1,0:T(8,128)S(1)} %get-tuple-element.6), channel_id=1, source_target_pairs={{0,29},{1,30},{2,31},{3,32},{4,33},{5,34},{6,35},{7,36},{8,37},{9,... | collective-permute-start | bytes 73736
  793.9 20.1 %collective-permute-start.35 = (f32[24,256]{1,0:T(8,128)S(1)}, f32[24,256]{1,0:T(8,128)S(1)}, u32[]{:S(2)}, u32[]{:S(2)}) collective-permute-start(f32[24,256]{1,0:T(8,128)S(1)} %get-tuple-element.6), channel_id=1, source_target_pairs={{0,30},{1,31},{2,32},{3,33},{4,34},{5,35},{6,36},{7,37},{8,38},{9,... | collective-permute-start | bytes 73736
  803.6 13.0 %collective-permute-start.36 = (f32[24,256]{1,0:T(8,128)S(1)}, f32[24,256]{1,0:T(8,128)S(1)}, u32[]{:S(2)}, u32[]{:S(2)}) collective-permute-start(f32[24,256]{1,0:T(8,128)S(1)} %get-tuple-element.6), channel_id=1, source_target_pairs={{0,31},{1,32},{2,33},{3,34},{4,35},{5,36},{6,37},{7,38},{8,39},{9,... | collective-permute-start | bytes 73736
  804.9 11.7 %collective-permute-start.6 = (f32[24,256]{1,0:T(8,128)S(1)}, f32[24,256]{1,0:T(8,128)S(1)}, u32[]{:S(2)}, u32[]{:S(2)}) collective-permute-start(f32[24,256]{1,0:T(8,128)S(1)} %get-tuple-element.6), channel_id=1, source_target_pairs={{0,1},{1,2},{2,3},{3,4},{4,5},{5,6},{6,7},{7,8},{8,9},{9,10},{10,1... | collective-permute-start | bytes 73736
  (82 other events, 954.8 us)
Sparse Core Ops, SparseCore 0:
  9.7 209.9 all-gather.2
